TPU v7x, 32 devices: a whole 2x2x4 slice. The times are simulated.
32 devices in a mesh: dp: 8 (over y, x, core), space: 4 (over z).
Axes of the slice: x: 2, y: 2, z: 4, core: 2. Of those that a mesh axis runs over, the one named last changes fastest.
Arguments:
- volume: bfloat16 [8, 8, 8, 8, 512], P('dp', 'space'), may hold values from -6 to 6
- conv_one: bfloat16 [3, 3, 3, 512, 256], P(None, None, None, 'dp'), may hold values from -0.125 to 0.125
- mix_one: bfloat16 [256, 256], P('dp'), may hold values from -0.375 to 0.375
- conv_two: bfloat16 [3, 3, 3, 256, 128], P(None, None, None, 'dp'), may hold values from -0.1875 to 0.1875
- mix_two: bfloat16 [128, 128], P('dp'), may hold values from -0.5 to 0.5
Outputs:
- decoded: bfloat16 [8, 32, 32, 32, 128], P('dp', 'space')
All inputs are finite; a program needn't handle non-finite values.
Results may differ from a plain program's by a relative error of at most 0.007.
Values may be sent and summed in bfloat16 or wider, within the bound.
A program may use at most 64 MiB of HBM per device.

v0:
```python
import jax
import jax.numpy as jnp
from jax import lax
from jax.sharding import PartitionSpec as P

PHASE_TAPS = (((1, 0),), ((2, 0), (0, 1)))


def shifted(block, axis, distance):
    devices = range(lax.axis_size(axis))
    route = [(i - distance, i) for i in devices if i - distance in devices]
    return lax.ppermute(block, axis, route)


def phase_sum(padded, weight, planes, height, breadth, depth_taps):
    chans_in = padded.shape[-1]
    chans_out = weight.shape[-1]
    groups = []
    for taps_depth in depth_taps:
        for taps_rows in PHASE_TAPS:
            for taps_cols in PHASE_TAPS:
                total = None
                for depth_tap, depth_shift in taps_depth:
                    for row_tap, row_shift in taps_rows:
                        for col_tap, col_shift in taps_cols:
                            piece = padded[
                                depth_shift : depth_shift + planes,
                                row_shift : row_shift + height,
                                col_shift : col_shift + breadth,
                            ]
                            term = jnp.dot(
                                piece.reshape(-1, chans_in),
                                weight[depth_tap, row_tap, col_tap],
                                preferred_element_type=jnp.float32,
                            )
                            total = term if total is None else total + term
                groups.append(total)
    return jnp.stack(groups).reshape(len(depth_taps), 2, 2, planes, height, breadth, chans_out)


def alternate(phased):
    planes, height, breadth, chans = phased.shape[3:]
    return jnp.transpose(phased, (3, 0, 4, 1, 5, 2, 6)).reshape(
        2 * planes, 2 * height, 2 * breadth, chans
    )


def expand(field, weight, first):
    planes, height, breadth, chans = field.shape
    if first:
        plane = shifted(field[0:1], "space", -1)
    else:
        plane = shifted(field[0:1], "space", -1)
    padded = jnp.pad(jnp.concatenate([field, plane], 0), ((0, 0), (0, 1), (0, 1), (0, 0)))
    phased = phase_sum(padded, weight, planes, height, breadth, PHASE_TAPS)
    return alternate(phased)


def finish(conv, mixing):
    act = jax.nn.silu(conv).astype(jnp.bfloat16)
    mixed = jnp.dot(act.reshape(-1, act.shape[-1]), mixing, preferred_element_type=jnp.float32)
    return mixed.astype(jnp.bfloat16).reshape(conv.shape[:-1] + (mixing.shape[1],))


def per_device(volume, conv_one, mix_one, conv_two, mix_two):
    field = volume[0]
    kernel_one, mixing_one = (
        lax.all_gather(conv_one, "dp", axis=3, tiled=True),
        lax.all_gather(mix_one, "dp", axis=0, tiled=True),
    )
    upper = finish(expand(field, kernel_one, True), mixing_one)
    kernel_two, mixing_two = (
        lax.all_gather(conv_two, "dp", axis=3, tiled=True),
        lax.all_gather(mix_two, "dp", axis=0, tiled=True),
    )
    decoded = finish(expand(upper, kernel_two, False), mixing_two)
    return decoded[None]


def solution(mesh):
    return jax.shard_map(
        per_device,
        mesh=mesh,
        in_specs=(
            P("dp", "space", None, None, None),
            P(None, None, None, "dp", None),
            P("dp", None),
            P(None, None, None, "dp", None),
            P("dp", None),
        ),
        out_specs=P("dp", "space", None, None, None),
        check_vma=False,
    )
```

profile of v0, /device:TPU:0, one launch (start us, length us, event | category | flops | bytes accessed | tf_op | source)
XLA Modules:
  0.0 114.8 jit_solution(14823665278782194715)
XLA Ops:
  6.5 0.7 all-gather.3.cloned.1.call-update
  7.3 0.8 slice_bitcast_fusion.108
  8.2 1.3 %collective-permute-start = (bf16[1,8,8,512]{3,2,1,0:T(8,128)(2,1)S(1)}, bf16[1,8,8,512]{3,2,1,0:T(8,128)(2,1)S(1)}, u32[]{:S(2)}, u32[]{:S(2)}) collective-permute-start(bf16[1,8,8,512]{3,2,1,0:T(8,128)(2,1)S(1)} %slice_bitcast_fusion.108), channel_id=1, source_target_pairs={{1,0},{2,1},{3,2},{5,4},{6,5},{7,6},{9,8},{10,9},{11,10},{13,12},{... | collective-permute-start | bytes 196616 | tf_op jit(solution)/shard_map/ppermute | solution.py:12
  9.5 10.7 %all_gather.15 = bf16[128,128]{1,0:T(8,128)(2,1)S(1)} all-gather(bf16[16,128]{1,0:T(8,128)(2,1)} %param.9), channel_id=1, replica_groups=mesh['dp'=8,'space'=4] {'dp'}, dimensions={0}, use_global_device_ids=true | all-gather | bytes 36864 | tf_op jit(solution)/shard_map/all_gather | solution.py:74
  20.1 9.4 %all_gather.13 = bf16[256,256]{1,0:T(8,128)(2,1)S(1)} all-gather(bf16[32,256]{1,0:T(8,128)(2,1)} %param.7), channel_id=1, replica_groups=mesh['dp'=8,'space'=4] {'dp'}, dimensions={0}, use_global_device_ids=true | all-gather | bytes 147456 | tf_op jit(solution)/shard_map/all_gather | solution.py:69
  29.5 0.9 pad_maximum_fusion.1
  30.5 0.9 fusion.38
  31.3 30.0 %all-gather.3.cloned.1.call-done = bf16[3,3,3,512,256]{4,3,2,1,0:T(8,128)(2,1)} async-done(((bf16[3,3,3,64,256]{4,3,2,1,0:T(8,128)(2,1)}), bf16[3,3,3,512,256]{4,3,2,1,0:T(8,128)(2,1)}) %all-gather.3.cloned.1.call-update) | async-done | bytes 7077904 | tf_op jit(solution)/shard_map/all_gather | solution.py:68
  61.4 1.3 %fusion.29 = f32[8,128,256]{2,1,0:T(8,128)S(1)} fusion(bf16[128,512]{1,0:T(8,128)(2,1)} %bitcast.315, bf16[3,3,3,512,256]{4,3,2,1,0:T(8,128)(2,1)} %all-gather.3.cloned.1.call-done), kind=kOutput, calls=%fused_computation.78 | convolution fusion | flops 33554432 | bytes 524288 | tf_op jit(solution)/shard_map/dot_general | solution.py:31
  62.7 1.5 %fusion.37 = f32[128,256]{1,0:T(8,128)S(1)} fusion(bf16[128,512]{1,0:T(8,128)(2,1)} %bitcast.316, bf16[3,3,3,512,256]{4,3,2,1,0:T(8,128)(2,1)} %all-gather.3.cloned.1.call-done), kind=kOutput, calls=%fused_computation.123 | convolution fusion | flops 33554432 | bytes 524288 | tf_op jit(solution)/shard_map/dot_general | solution.py:31
  64.2 1.1 fusion.36
  65.4 1.1 fusion.35
  66.5 1.1 fusion.33
  67.7 1.1 fusion.32
  68.8 1.1 fusion.31
  70.0 1.1 convolution_add_fusion.35
  71.1 1.1 convolution_add_fusion.31
  72.3 1.1 convolution_add_fusion.34
  73.4 1.1 convolution_add_fusion.28
  74.6 1.1 convolution_add_fusion.30
  75.7 1.1 convolution_add_fusion.27
  79.6 0.8 copy.9
  80.5 0.7 reshape.55
  81.2 0.4 convolution_convert_fusion.1
  81.6 1.5 %collective-permute-start.1 = (bf16[1,16,16,256]{3,2,1,0:T(8,128)(2,1)S(1)}, bf16[1,16,16,256]{3,2,1,0:T(8,128)(2,1)S(1)}, u32[]{:S(2)}, u32[]{:S(2)}) collective-permute-start(bf16[1,16,16,256]{3,2,1,0:T(8,128)(2,1)S(1)} %bitcast.365), channel_id=1, source_target_pairs={{1,0},{2,1},{3,2},{5,4},{6,5},{7,6},{9,8},{10,9},{11,10},{13,12},{... | collective-permute-start | bytes 393224 | tf_op jit(solution)/shard_map/ppermute | solution.py:12
  83.1 7.0 %all-gather.5.cloned.1.call-done = bf16[3,3,3,256,128]{4,3,2,1,0:T(8,128)(2,1)} async-done(((bf16[3,3,3,32,128]{4,3,2,1,0:T(8,128)(2,1)}), bf16[3,3,3,256,128]{4,3,2,1,0:T(8,128)(2,1)}) %all-gather.5.cloned.1.call-update) | async-done | bytes 1769488 | tf_op jit(solution)/shard_map/all_gather | solution.py:73
  90.1 1.2 %fusion = f32[8,1024,128]{2,1,0:T(8,128)S(1)} fusion(bf16[1024,256]{1,0:T(8,128)(2,1)S(1)} %convolution_convert_fusion.1, bf16[3,3,3,256,128]{4,3,2,1,0:T(8,128)(2,1)} %all-gather.5.cloned.1.call-done), kind=kOutput, calls=%fused_computation.10 | convolution fusion | flops 67108864 | bytes 1114112 | tf_op jit(solution)/shard_map/dot_general | solution.py:31
  91.3 1.1 fusion.45
  92.5 1.1 fusion.44
  93.6 1.1 fusion.43
  96.0 0.3 pad_slice_fusion
  96.4 0.3 convolution_add_fusion.16
  96.7 0.3 convolution_add_fusion.12
  97.3 0.3 convolution_add_fusion.9
  97.6 0.3 convolution_add_fusion.11
  97.9 0.3 convolution_add_fusion.8
  98.2 0.3 convolution_add_fusion.6
  98.8 0.3 convolution_add_fusion.4
  99.1 0.3 convolution_add_fusion.3
  99.4 0.3 fusion.14
  99.7 0.3 fusion.12
  100.3 0.3 fusion.8
  100.7 0.3 convolution_add_fusion.2
  101.0 0.3 fusion.6
  101.3 0.3 convolution_add_fusion.1
  101.9 0.3 fusion.2
  102.2 3.3 %copy.7 = f32[2,2,2,4,16,16,128]{6,2,5,1,4,0,3:T(2,128)S(1)} copy(f32[2,2,2,4,16,16,128]{6,5,4,3,2,1,0:T(8,128)S(1)} %bitcast.335) | data formatting | bytes 8388608 | tf_op jit(solution)/shard_map/reshape | solution.py:38
  105.5 2.5 %convolution_convert_fusion = bf16[8192,128]{1,0:T(8,128)(2,1)} fusion(bf16[128,128]{1,0:T(8,128)(2,1)S(1)} %all_gather.15, f32[8192,128]{1,0:T(8,128)S(1)} %bitcast.342), kind=kOutput, calls=%fused_computation | convolution fusion | flops 274726912 | bytes 6324224 | tf_op jit(solution)/shard_map/dot_general | solution.py:61
  (37 shorter events, 5.3 us)
Async XLA Ops:
  6.5 57.7 %copy-start = (bf16[1,2,8,8,512]{4,3,2,1,0:T(8,128)(2,1)S(1)}, bf16[1,2,8,8,512]{4,3,2,1,0:T(8,128)(2,1)}, u32[]{:S(2)}) copy-start(bf16[1,2,8,8,512]{4,3,2,1,0:T(8,128)(2,1)} %param.5) | copy-start | bytes 393220
  6.5 54.8 %all-gather.3.cloned.1.call-start = ((), (), s32[]{:S(2)}) async-start(), calls=%async_computation | async-start | bytes 7962624 | tf_op jit(solution)/shard_map/all_gather | solution.py:68
  7.3 82.8 %all-gather.5.cloned.1.call-start = ((), (), s32[]{:S(2)}) async-start(), calls=%async_computation.1 | async-start | bytes 1990656 | tf_op jit(solution)/shard_map/all_gather | solution.py:73
  8.2 21.3 %collective-permute-start = (bf16[1,8,8,512]{3,2,1,0:T(8,128)(2,1)S(1)}, bf16[1,8,8,512]{3,2,1,0:T(8,128)(2,1)S(1)}, u32[]{:S(2)}, u32[]{:S(2)}) collective-permute-start(bf16[1,8,8,512]{3,2,1,0:T(8,128)(2,1)S(1)} %slice_bitcast_fusion.108), channel_id=1, source_target_pairs={{1,0},{2,1},{3,2},{5,4},{6,5},{7,6},{9,8},{10,9},{11,10},{13,12},{... | collective-permute-start | bytes 196616 | tf_op jit(solution)/shard_map/ppermute | solution.py:12
  61.4 15.5 %copy-start.1 = (bf16[3,3,3,512,256]{4,3,2,1,0:T(8,128)(2,1)S(1)}, bf16[3,3,3,512,256]{4,3,2,1,0:T(8,128)(2,1)}, u32[]{:S(2)}) copy-start(bf16[3,3,3,512,256]{4,3,2,1,0:T(8,128)(2,1)} %all-gather.3.cloned.1.call-done) | copy-start | bytes 21233668
  81.6 14.3 %collective-permute-start.1 = (bf16[1,16,16,256]{3,2,1,0:T(8,128)(2,1)S(1)}, bf16[1,16,16,256]{3,2,1,0:T(8,128)(2,1)S(1)}, u32[]{:S(2)}, u32[]{:S(2)}) collective-permute-start(bf16[1,16,16,256]{3,2,1,0:T(8,128)(2,1)S(1)} %bitcast.365), channel_id=1, source_target_pairs={{1,0},{2,1},{3,2},{5,4},{6,5},{7,6},{9,8},{10,9},{11,10},{13,12},{... | collective-permute-start | bytes 393224 | tf_op jit(solution)/shard_map/ppermute | solution.py:12
  90.1 4.7 %copy-start.2 = (bf16[3,3,3,256,128]{4,3,2,1,0:T(8,128)(2,1)S(1)}, bf16[3,3,3,256,128]{4,3,2,1,0:T(8,128)(2,1)}, u32[]{:S(2)}) copy-start(bf16[3,3,3,256,128]{4,3,2,1,0:T(8,128)(2,1)} %all-gather.5.cloned.1.call-done) | copy-start | bytes 5308420
Sparse Core Ops, SparseCore 0:
  9.3 52.0 all-gather.2
  63.2 26.7 all-gather.4
where the time goes:
time: 116 us; the launch traced here: 115 us
  waiting for transfers between devices  37.7 us (33%)
  matrix products  32.5 us (28%)
  blocking collectives  20 us (17%)
  between operations  13.8 us (12%)
  local copies, waits for them, and re-layouts  6.06 us (5%)
  starting transfers between devices  2.79 us (2%)
  other arithmetic  1.89 us (2%)
    all_gather x1, waiting for transfers between devices, per_device(): lax.all_gather(conv_one, 'dp', axis=3, tiled=True)  30 us
    dot_general x54, matrix products, phase_sum(): jnp.dot(piece.reshape(-1, chans_in), weight[depth_tap, row_tap, col_tap],...  29.6 us
    all_gather x1, blocking collectives, per_device(): lax.all_gather(mix_two, 'dp', axis=0, tiled=True)  10.7 us
    all_gather x1, blocking collectives, per_device(): lax.all_gather(mix_one, 'dp', axis=0, tiled=True)  9.36 us
    all_gather x1, waiting for transfers between devices, per_device(): lax.all_gather(conv_two, 'dp', axis=3, tiled=True)  6.95 us
    reshape x2, local copies, waits for them, and re-layouts, phase_sum(): jnp.stack(groups)  4.09 us
    dot_general x2, matrix products, finish(): jnp.dot(act.reshape(-1, act.shape[-1]), mixing, preferred_element_type=jn...  2.96 us
    ppermute x2, starting transfers between devices, shifted(): return lax.ppermute(block, axis, route)  2.75 us
  transfers between devices with their start and end apart: 4, of which 2 were waited for; matrix products, arithmetic and copies ran while one was open for 25% of the time, Pallas kernels for 0%

commit v1 on v0

--- a/solution.py
+++ b/solution.py
@@ -4,6 +4,28 @@
 from jax.sharding import PartitionSpec as P
 
 PHASE_TAPS = (((1, 0),), ((2, 0), (0, 1)))
+
+
+def in_order(pieces, dim):
+    lengths = list(pieces.shape[1:])
+    lengths[dim] *= pieces.shape[0]
+    return jnp.moveaxis(pieces, 0, dim).reshape(lengths)
+
+
+def ring_gather(x, axis, dim):
+    size = lax.axis_size(axis)
+    pairs = [(i, (i + 1) % size) for i in range(size)]
+    back = [(b, a) for a, b in pairs]
+    lower, upper = ([], [])
+    for turn in range(size - 1):
+        if turn % 2 == 0:
+            lower.append(lax.ppermute(lower[-1] if lower else x, axis, pairs))
+        else:
+            upper.append(lax.ppermute(upper[-1] if upper else x, axis, back))
+    blocks = jnp.stack([*lower[::-1], x, *upper])
+    shift = lax.axis_index(axis) - len(lower)
+    blocks = blocks[(jnp.arange(size) - shift) % size]
+    return in_order(blocks, dim)
 
 
 def shifted(block, axis, distance):
@@ -66,7 +88,7 @@
     field = volume[0]
     kernel_one, mixing_one = (
         lax.all_gather(conv_one, "dp", axis=3, tiled=True),
-        lax.all_gather(mix_one, "dp", axis=0, tiled=True),
+        ring_gather(mix_one, "dp", 0),
     )
     upper = finish(expand(field, kernel_one, True), mixing_one)
     kernel_two, mixing_two = (

time: 116 us -> 115 us (level)
  blocking collectives: 20 us -> 10 us
  starting transfers between devices: 2.79 us -> 10.3 us
  waiting for transfers between devices: 37.7 us -> 39.1 us
    all_gather x1 -> x0, blocking collectives: 9.36 us -> none  [per_device(): lax.all_gather(mix_one, 'dp', axis=0, tiled=True)]
    ppermute x0 -> x7, starting transfers between devices: none -> 7.53 us  [the longest x3 7.01 us: ring_gather(): upper.append(lax.ppermute(upper[-1] if upper else x, axis, back))]
    ppermute x0 -> x7, waiting for transfers between devices: none -> 4.82 us  [the longest x4 4.81 us: ring_gather(): lower.append(lax.ppermute(lower[-1] if lower else x, axis, pairs))]
    all_gather x1, waiting for transfers between devices: 30 us -> 26 us  [per_device(): lax.all_gather(conv_one, 'dp', axis=3, tiled=True)]
    reshape x2 -> x1, local copies, waits for them, and re-layouts: 4.09 us -> 3.28 us  [phase_sum(): jnp.stack(groups)]
  transfers between devices with their start and end apart: 4 -> 11, of which waited for: 2 -> 5; matrix products, arithmetic and copies ran while one was open for 25% -> 25% of each run, Pallas kernels for 0% -> 0%
where the time goes in v1:
time: 115 us
  waiting for transfers between devices  39.1 us (34%)
  matrix products  32.4 us (28%)
  between operations  13.9 us (12%)
  starting transfers between devices  10.3 us (9%)
  blocking collectives  10 us (9%)
  local copies, waits for them, and re-layouts  6.56 us (6%)
  other arithmetic  2.2 us (2%)
    dot_general x54, matrix products, phase_sum(): jnp.dot(piece.reshape(-1, chans_in), weight[depth_tap, row_tap, col_tap],...  29.6 us
    all_gather x1, waiting for transfers between devices, per_device(): lax.all_gather(conv_one, 'dp', axis=3, tiled=True)  26 us
    all_gather x1, blocking collectives, per_device(): lax.all_gather(mix_two, 'dp', axis=0, tiled=True)  10 us
    all_gather x1, waiting for transfers between devices, per_device(): lax.all_gather(conv_two, 'dp', axis=3, tiled=True)  7.58 us
    ppermute x3, starting transfers between devices, ring_gather(): upper.append(lax.ppermute(upper[-1] if upper else x, axis, back))  7.01 us
    ppermute x4, waiting for transfers between devices, ring_gather(): lower.append(lax.ppermute(lower[-1] if lower else x, axis, pairs))  4.81 us
    reshape x1, local copies, waits for them, and re-layouts, phase_sum(): jnp.stack(groups)  3.28 us
    dot_general x2, matrix products, finish(): jnp.dot(act.reshape(-1, act.shape[-1]), mixing, preferred_element_type=jn...  2.83 us
  transfers between devices with their start and end apart: 11, of which 5 were waited for; matrix products, arithmetic and copies ran while one was open for 25% of the time, Pallas kernels for 0%

profile of v1, /device:TPU:0, one launch (start us, length us, event | category | flops | bytes accessed | tf_op | source)
XLA Modules:
  0.0 114.6 jit_solution(9186889178884043747)
XLA Ops:
  6.5 0.7 all-gather.3.cloned.1.call-update
  7.3 0.5 collective-permute-start.1
  7.8 2.9 %collective-permute-start.5 = (bf16[32,256]{1,0:T(8,128)(2,1)}, bf16[32,256]{1,0:T(8,128)(2,1)S(1)}, u32[]{:S(2)}, u32[]{:S(2)}) collective-permute-start(bf16[32,256]{1,0:T(8,128)(2,1)} %param.7), channel_id=1, source_target_pairs={{4,0},{8,4},{12,8},{16,12},{20,16},{24,20},{28,24},{0,28},{5,1},{9... | collective-permute-start | bytes 49160 | tf_op jit(solution)/shard_map/ppermute | solution.py:24
  10.8 1.6 %collective-permute-done.1 = bf16[32,256]{1,0:T(8,128)(2,1)S(1)} collective-permute-done((bf16[32,256]{1,0:T(8,128)(2,1)}, bf16[32,256]{1,0:T(8,128)(2,1)S(1)}, u32[]{:S(2)}, u32[]{:S(2)}) %collective-permute-start.1) | collective-permute-done | bytes 16416 | tf_op jit(solution)/shard_map/ppermute | solution.py:22
  12.3 0.8 slice_bitcast_fusion.108
  13.2 1.3 %collective-permute-start = (bf16[1,8,8,512]{3,2,1,0:T(8,128)(2,1)S(1)}, bf16[1,8,8,512]{3,2,1,0:T(8,128)(2,1)S(1)}, u32[]{:S(2)}, u32[]{:S(2)}) collective-permute-start(bf16[1,8,8,512]{3,2,1,0:T(8,128)(2,1)S(1)} %slice_bitcast_fusion.108), channel_id=1, source_target_pairs={{1,0},{2,1},{3,2},{5,4},{6,5},{7,6},{9,8},{10,9},{11,10},{13,12},{... | collective-permute-start | bytes 196616 | tf_op jit(solution)/shard_map/ppermute | solution.py:34
  14.5 1.9 %collective-permute-done.2 = bf16[32,256]{1,0:T(8,128)(2,1)S(1)} collective-permute-done((bf16[32,256]{1,0:T(8,128)(2,1)S(1)}, bf16[32,256]{1,0:T(8,128)(2,1)S(1)}, u32[]{:S(2)}, u32[]{:S(2)}) %collective-permute-start.2) | collective-permute-done | bytes 16416 | tf_op jit(solution)/shard_map/ppermute | solution.py:22
  16.4 2.7 %collective-permute-start.6 = (bf16[32,256]{1,0:T(8,128)(2,1)S(1)}, bf16[32,256]{1,0:T(8,128)(2,1)S(1)}, u32[]{:S(2)}, u32[]{:S(2)}) collective-permute-start(bf16[32,256]{1,0:T(8,128)(2,1)S(1)} %collective-permute-done.5), channel_id=1, source_target_pairs={{4,0},{8,4},{12,8},{16,12},{20,16},{24,20},{28,24},{0,28},{5,1},{9... | collective-permute-start | bytes 49160 | tf_op jit(solution)/shard_map/ppermute | solution.py:24
  19.1 1.3 %collective-permute-done.3 = bf16[32,256]{1,0:T(8,128)(2,1)S(1)} collective-permute-done((bf16[32,256]{1,0:T(8,128)(2,1)S(1)}, bf16[32,256]{1,0:T(8,128)(2,1)S(1)}, u32[]{:S(2)}, u32[]{:S(2)}) %collective-permute-start.3) | collective-permute-done | bytes 16416 | tf_op jit(solution)/shard_map/ppermute | solution.py:22
  20.5 10.0 %all_gather.11 = bf16[128,128]{1,0:T(8,128)(2,1)S(1)} all-gather(bf16[16,128]{1,0:T(8,128)(2,1)} %param.9), channel_id=1, replica_groups=mesh['dp'=8,'space'=4] {'dp'}, dimensions={0}, use_global_device_ids=true | all-gather | bytes 36864 | tf_op jit(solution)/shard_map/all_gather | solution.py:96
  30.5 1.4 %collective-permute-start.7 = (bf16[32,256]{1,0:T(8,128)(2,1)S(1)}, bf16[32,256]{1,0:T(8,128)(2,1)S(1)}, u32[]{:S(2)}, u32[]{:S(2)}) collective-permute-start(bf16[32,256]{1,0:T(8,128)(2,1)S(1)} %collective-permute-done.6), channel_id=1, source_target_pairs={{4,0},{8,4},{12,8},{16,12},{20,16},{24,20},{28,24},{0,28},{5,1},{9... | collective-permute-start | bytes 49160 | tf_op jit(solution)/shard_map/ppermute | solution.py:24
  31.9 0.7 constant_dynamic-update-slice_fusion.3
  32.7 0.9 pad_maximum_fusion.1
  33.7 0.6 gather_fusion
  34.2 0.9 fusion.42
  35.1 26.0 %all-gather.3.cloned.1.call-done = bf16[3,3,3,512,256]{4,3,2,1,0:T(8,128)(2,1)} async-done(((bf16[3,3,3,64,256]{4,3,2,1,0:T(8,128)(2,1)}), bf16[3,3,3,512,256]{4,3,2,1,0:T(8,128)(2,1)}) %all-gather.3.cloned.1.call-update) | async-done | bytes 7077904 | tf_op jit(solution)/shard_map/all_gather | solution.py:90
  61.1 1.4 %fusion.29 = f32[8,128,256]{2,1,0:T(8,128)S(1)} fusion(bf16[128,512]{1,0:T(8,128)(2,1)} %bitcast.345, bf16[3,3,3,512,256]{4,3,2,1,0:T(8,128)(2,1)} %all-gather.3.cloned.1.call-done), kind=kOutput, calls=%fused_computation.79 | convolution fusion | flops 33554432 | bytes 524288 | tf_op jit(solution)/shard_map/dot_general | solution.py:53
  62.5 1.5 %fusion.41 = f32[128,256]{1,0:T(8,128)S(1)} fusion(bf16[128,512]{1,0:T(8,128)(2,1)} %bitcast.346, bf16[3,3,3,512,256]{4,3,2,1,0:T(8,128)(2,1)} %all-gather.3.cloned.1.call-done), kind=kOutput, calls=%fused_computation.128 | convolution fusion | flops 33554432 | bytes 524288 | tf_op jit(solution)/shard_map/dot_general | solution.py:53
  64.0 1.1 fusion.40
  65.1 1.1 fusion.39
  66.3 1.1 fusion.37
  67.4 1.1 fusion.36
  68.6 1.1 %fusion.35 = f32[128,256]{1,0:T(8,128)S(1)} fusion(bf16[128,512]{1,0:T(8,128)(2,1)S(1)} %bitcast.351, bf16[3,3,3,512,256]{4,3,2,1,0:T(8,128)(2,1)} %all-gather.3.cloned.1.call-done), kind=kOutput, calls=%fused_computation.104 | convolution fusion | flops 33554432 | bytes 524288 | tf_op jit(solution)/shard_map/dot_general | solution.py:53
  69.7 1.1 %convolution_add_fusion.35 = f32[128,256]{1,0:T(8,128)S(1)} fusion(f32[128,256]{1,0:T(8,128)S(1)} %fusion.39, bf16[128,512]{1,0:T(8,128)(2,1)S(1)} %bitcast.377, bf16[3,3,3,512,256]{4,3,2,1,0:T(8,128)(2,1)} %all-gather.3.cloned.1.call-done), kind=kOutput, calls=%fused_computation.71 | convolution fusion | flops 33587200 | bytes 655360 | tf_op jit(solution)/shard_map/dot_general | solution.py:53
  70.9 1.1 convolution_add_fusion.31
  72.0 1.1 convolution_add_fusion.34
  73.2 1.1 convolution_add_fusion.28
  74.3 1.1 convolution_add_fusion.30
  75.5 1.1 convolution_add_fusion.27
  79.7 0.5 copy.11
  80.7 1.5 %collective-permute-start.8 = (bf16[1,16,16,256]{3,2,1,0:T(8,128)(2,1)S(1)}, bf16[1,16,16,256]{3,2,1,0:T(8,128)(2,1)S(1)}, u32[]{:S(2)}, u32[]{:S(2)}) collective-permute-start(bf16[1,16,16,256]{3,2,1,0:T(8,128)(2,1)S(1)} %bitcast.395), channel_id=1, source_target_pairs={{1,0},{2,1},{3,2},{5,4},{6,5},{7,6},{9,8},{10,9},{11,10},{13,12},{... | collective-permute-start | bytes 393224 | tf_op jit(solution)/shard_map/ppermute | solution.py:34
  82.2 7.6 %all-gather.5.cloned.1.call-done = bf16[3,3,3,256,128]{4,3,2,1,0:T(8,128)(2,1)} async-done(((bf16[3,3,3,32,128]{4,3,2,1,0:T(8,128)(2,1)}), bf16[3,3,3,256,128]{4,3,2,1,0:T(8,128)(2,1)}) %all-gather.5.cloned.1.call-update) | async-done | bytes 1769488 | tf_op jit(solution)/shard_map/all_gather | solution.py:95
  89.8 1.2 %fusion = f32[8,1024,128]{2,1,0:T(8,128)S(1)} fusion(bf16[1024,256]{1,0:T(8,128)(2,1)S(1)} %convolution_convert_fusion.1, bf16[3,3,3,256,128]{4,3,2,1,0:T(8,128)(2,1)} %all-gather.5.cloned.1.call-done), kind=kOutput, calls=%fused_computation.11 | convolution fusion | flops 67108864 | bytes 1114112 | tf_op jit(solution)/shard_map/dot_general | solution.py:53
  91.1 1.1 fusion.49
  92.2 1.1 fusion.48
  93.3 1.1 fusion.47
  95.8 0.3 pad_slice_fusion
  96.4 0.3 convolution_add_fusion.12
  97.4 0.3 convolution_add_fusion.11
  97.7 0.3 convolution_add_fusion.8
  98.0 0.3 convolution_add_fusion.6
  98.9 0.3 convolution_add_fusion.3
  99.2 0.3 fusion.14
  99.5 0.3 fusion.12
  100.7 0.3 fusion.6
  101.0 0.3 convolution_add_fusion.1
  101.9 3.3 %copy.12 = f32[2,2,2,4,16,16,128]{6,2,5,1,4,0,3:T(2,128)S(1)} copy(f32[2,2,2,4,16,16,128]{6,5,4,3,2,1,0:T(8,128)S(1)} %bitcast.365) | data formatting | bytes 8388608 | tf_op jit(solution)/shard_map/reshape | solution.py:60
  105.2 2.5 %convolution_convert_fusion = bf16[8192,128]{1,0:T(8,128)(2,1)} fusion(bf16[128,128]{1,0:T(8,128)(2,1)S(1)} %all_gather.11, f32[8192,128]{1,0:T(8,128)S(1)} %bitcast.372), kind=kOutput, calls=%fused_computation.1 | convolution fusion | flops 274726912 | bytes 6324224 | tf_op jit(solution)/shard_map/dot_general | solution.py:83
  (62 shorter events, 7.9 us)
Async XLA Ops:
  6.5 57.4 %copy-start = (bf16[1,2,8,8,512]{4,3,2,1,0:T(8,128)(2,1)S(1)}, bf16[1,2,8,8,512]{4,3,2,1,0:T(8,128)(2,1)}, u32[]{:S(2)}) copy-start(bf16[1,2,8,8,512]{4,3,2,1,0:T(8,128)(2,1)} %param.5) | copy-start | bytes 393220
  6.5 54.6 %all-gather.3.cloned.1.call-start = ((), (), s32[]{:S(2)}) async-start(), calls=%async_computation | async-start | bytes 7962624 | tf_op jit(solution)/shard_map/all_gather | solution.py:90
  7.3 82.5 %all-gather.5.cloned.1.call-start = ((), (), s32[]{:S(2)}) async-start(), calls=%async_computation.1 | async-start | bytes 1990656 | tf_op jit(solution)/shard_map/all_gather | solution.py:95
  7.3 5.0 %collective-permute-start.1 = (bf16[32,256]{1,0:T(8,128)(2,1)}, bf16[32,256]{1,0:T(8,128)(2,1)S(1)}, u32[]{:S(2)}, u32[]{:S(2)}) collective-permute-start(bf16[32,256]{1,0:T(8,128)(2,1)} %param.7), channel_id=1, source_target_pairs={{0,4},{4,8},{8,12},{12,16},{16,20},{20,24},{24,28},{28,0},{1,5},{5... | collective-permute-start | bytes 49160 | tf_op jit(solution)/shard_map/ppermute | solution.py:22
  7.8 8.6 %collective-permute-start.5 = (bf16[32,256]{1,0:T(8,128)(2,1)}, bf16[32,256]{1,0:T(8,128)(2,1)S(1)}, u32[]{:S(2)}, u32[]{:S(2)}) collective-permute-start(bf16[32,256]{1,0:T(8,128)(2,1)} %param.7), channel_id=1, source_target_pairs={{4,0},{8,4},{12,8},{16,12},{20,16},{24,20},{28,24},{0,28},{5,1},{9... | collective-permute-start | bytes 49160 | tf_op jit(solution)/shard_map/ppermute | solution.py:24
  12.3 4.1 %collective-permute-start.2 = (bf16[32,256]{1,0:T(8,128)(2,1)S(1)}, bf16[32,256]{1,0:T(8,128)(2,1)S(1)}, u32[]{:S(2)}, u32[]{:S(2)}) collective-permute-start(bf16[32,256]{1,0:T(8,128)(2,1)S(1)} %collective-permute-done.1), channel_id=1, source_target_pairs={{0,4},{4,8},{8,12},{12,16},{16,20},{20,24},{24,28},{28,0},{1,5},{5... | collective-permute-start | bytes 49160 | tf_op jit(solution)/shard_map/ppermute | solution.py:22
  13.2 19.5 %collective-permute-start = (bf16[1,8,8,512]{3,2,1,0:T(8,128)(2,1)S(1)}, bf16[1,8,8,512]{3,2,1,0:T(8,128)(2,1)S(1)}, u32[]{:S(2)}, u32[]{:S(2)}) collective-permute-start(bf16[1,8,8,512]{3,2,1,0:T(8,128)(2,1)S(1)} %slice_bitcast_fusion.108), channel_id=1, source_target_pairs={{1,0},{2,1},{3,2},{5,4},{6,5},{7,6},{9,8},{10,9},{11,10},{13,12},{... | collective-permute-start | bytes 196616 | tf_op jit(solution)/shard_map/ppermute | solution.py:34
  16.4 4.1 %collective-permute-start.3 = (bf16[32,256]{1,0:T(8,128)(2,1)S(1)}, bf16[32,256]{1,0:T(8,128)(2,1)S(1)}, u32[]{:S(2)}, u32[]{:S(2)}) collective-permute-start(bf16[32,256]{1,0:T(8,128)(2,1)S(1)} %collective-permute-done.2), channel_id=1, source_target_pairs={{0,4},{4,8},{8,12},{12,16},{16,20},{20,24},{24,28},{28,0},{1,5},{5... | collective-permute-start | bytes 49160 | tf_op jit(solution)/shard_map/ppermute | solution.py:22
  16.4 14.1 %collective-permute-start.6 = (bf16[32,256]{1,0:T(8,128)(2,1)S(1)}, bf16[32,256]{1,0:T(8,128)(2,1)S(1)}, u32[]{:S(2)}, u32[]{:S(2)}) collective-permute-start(bf16[32,256]{1,0:T(8,128)(2,1)S(1)} %collective-permute-done.5), channel_id=1, source_target_pairs={{4,0},{8,4},{12,8},{16,12},{20,16},{24,20},{28,24},{0,28},{5,1},{9... | collective-permute-start | bytes 49160 | tf_op jit(solution)/shard_map/ppermute | solution.py:24
  20.5 11.4 %collective-permute-start.4 = (bf16[32,256]{1,0:T(8,128)(2,1)S(1)}, bf16[32,256]{1,0:T(8,128)(2,1)S(1)}, u32[]{:S(2)}, u32[]{:S(2)}) collective-permute-start(bf16[32,256]{1,0:T(8,128)(2,1)S(1)} %collective-permute-done.3), channel_id=1, source_target_pairs={{0,4},{4,8},{8,12},{12,16},{16,20},{20,24},{24,28},{28,0},{1,5},{5... | collective-permute-start | bytes 49160 | tf_op jit(solution)/shard_map/ppermute | solution.py:22
  30.5 3.1 %collective-permute-start.7 = (bf16[32,256]{1,0:T(8,128)(2,1)S(1)}, bf16[32,256]{1,0:T(8,128)(2,1)S(1)}, u32[]{:S(2)}, u32[]{:S(2)}) collective-permute-start(bf16[32,256]{1,0:T(8,128)(2,1)S(1)} %collective-permute-done.6), channel_id=1, source_target_pairs={{4,0},{8,4},{12,8},{16,12},{20,16},{24,20},{28,24},{0,28},{5,1},{9... | collective-permute-start | bytes 49160 | tf_op jit(solution)/shard_map/ppermute | solution.py:24
  61.1 15.5 %copy-start.1 = (bf16[3,3,3,512,256]{4,3,2,1,0:T(8,128)(2,1)S(1)}, bf16[3,3,3,512,256]{4,3,2,1,0:T(8,128)(2,1)}, u32[]{:S(2)}) copy-start(bf16[3,3,3,512,256]{4,3,2,1,0:T(8,128)(2,1)} %all-gather.3.cloned.1.call-done) | copy-start | bytes 21233668
  80.7 14.9 %collective-permute-start.8 = (bf16[1,16,16,256]{3,2,1,0:T(8,128)(2,1)S(1)}, bf16[1,16,16,256]{3,2,1,0:T(8,128)(2,1)S(1)}, u32[]{:S(2)}, u32[]{:S(2)}) collective-permute-start(bf16[1,16,16,256]{3,2,1,0:T(8,128)(2,1)S(1)} %bitcast.395), channel_id=1, source_target_pairs={{1,0},{2,1},{3,2},{5,4},{6,5},{7,6},{9,8},{10,9},{11,10},{13,12},{... | collective-permute-start | bytes 393224 | tf_op jit(solution)/shard_map/ppermute | solution.py:34
  89.8 4.7 %copy-start.2 = (bf16[3,3,3,256,128]{4,3,2,1,0:T(8,128)(2,1)S(1)}, bf16[3,3,3,256,128]{4,3,2,1,0:T(8,128)(2,1)}, u32[]{:S(2)}) copy-start(bf16[3,3,3,256,128]{4,3,2,1,0:T(8,128)(2,1)} %all-gather.5.cloned.1.call-done) | copy-start | bytes 5308420
Sparse Core Ops, SparseCore 0:
  9.3 51.7 all-gather.2
  63.0 26.7 all-gather.4
